TPU v7x, 768 devices: a whole 4x8x12 slice. The times are simulated.
768 devices in a mesh: lon: 48 (over y_hi, z), lat: 16 (over x, y_lo, core).
Axes of the slice: x: 4, y: 8 (y_hi: 4, y_lo: 2; y = y_hi * 2 + y_lo), z: 12, core: 2. Of those that a mesh axis runs over, the one named last changes fastest.
Arguments:
- tracers: float32 [4, 8, 256, 6144], P(None, None, 'lat', 'lon'), may hold values from -6 to 6
- east_speed: float32 [8, 256, 6144], P(None, 'lat', 'lon'), may hold values from -1.25 to 1.25
- north_speed: float32 [8, 256, 6144], P(None, 'lat', 'lon'), may hold values from -1.25 to 1.25
- mixing_coef: float32 [7, 256, 6144], P(None, 'lat', 'lon'), may hold values from 0.05 to 5
- ocean_mask: int32 [256, 6144], P('lat', 'lon'), may hold values 0 or 1
- fold_map: int32 [6144], P('lon'), may hold values from 0 to 6143, as said below
- atmos_state: float32 [4, 786432], P(None, ('lon', 'lat')), may hold values from -6 to 6
- atmos_coef: float32 [786432], P(('lon', 'lat')), may hold values from 0.1 to 1
- xgrid_cell: int32 [4718592], P(('lon', 'lat')), may hold values from 0 to 2047
- xgrid_atm: int32 [4718592], P(('lon', 'lat')), may hold values from 0 to 1023
- xgrid_owner: int32 [4718592, 1], P(('lon', 'lat')), may hold values from 0 to 47; in each aligned block of 6144 rows (0 to 6143, 6144 to 12287, ...) at most 256 rows name the same one
- xgrid_weight: float32 [4718592], P(('lon', 'lat')), may hold values from 0.2 to 1
Outputs:
- tracers_next: float32 [4, 8, 256, 6144], P(None, None, 'lat', 'lon')
Inputs may be any that keep to these rules, and one draw needn't show every extreme that they name: `fold_map`: the mirror longitude of each top-row point; applying it twice gives the identity, and no point is its own mirror. `xgrid_cell`: row * 128 + column of the ocean cell inside the tile that holds the list row. `xgrid_atm`: atmosphere cell inside the owner's block. `xgrid_owner`: longitude tile of the atmosphere owner, in the list row's latitude row; within the rows of one tile no owner appears more than 256 times. `ocean_mask`: 1 for ocean, 0 for land.
All inputs are finite; a program needn't handle non-finite values. No bound on the sum of `ocean_mask` on one device may be relied on, other than what follows from the above.
Results may differ from a plain program's by a relative error of at most 0.0003.
Values sent between devices are 32-bit elements; how exact they have to be, the bound alone decides.
A program may use at most 128 MiB of HBM per device.

v0:
```python
import jax
import jax.numpy as jnp
from jax import lax
from jax.experimental import pallas as pl
from jax.experimental.pallas import tpu as pltpu
from jax.sharding import PartitionSpec as P

flux_step = 0.5
LANES = 128
WIDE = 512


def pack_kernel(tr, es, ns, om, state, coef, gat, north, south, east, west):
    tracer_count, level_count, row_count, cols = tr.shape
    blocks = state.shape[1] // LANES
    for t in range(tracer_count):
        for h in range(blocks):
            gat[t * blocks + h : t * blocks + h + 1, :] = state[t : t + 1, h * LANES : (h + 1) * LANES]
    gat[tracer_count * blocks : (tracer_count + 1) * blocks, :] = coef[...]
    base = (tracer_count + 1) * blocks
    plane_count = tracer_count * level_count
    lane = lax.broadcasted_iota(jnp.int32, (row_count, cols), 1)
    mask = om[...].astype(jnp.float32)
    gat[base:, :] = jnp.zeros((gat.shape[0] - base, cols), jnp.float32)
    north[...] = jnp.zeros_like(north)
    south[...] = jnp.zeros_like(south)
    first = jnp.zeros((row_count, cols), jnp.float32)
    last = jnp.zeros((row_count, cols), jnp.float32)
    for p in range(plane_count + 1 + level_count):
        if p < plane_count:
            plane = tr[p // level_count, p % level_count]
            north_plane = plane
        elif p == plane_count:
            plane = mask
            north_plane = plane
        else:
            plane = es[p - plane_count - 1]
            north_plane = ns[p - plane_count - 1]
        north[p : p + 1, :] = north_plane[row_count - 1 : row_count, :]
        last = jnp.where(lane == p, plane[:, cols - 1 : cols], last)
        if p <= plane_count:
            gat[base + p : base + p + 1, :] = plane[row_count - 1 : row_count, :]
            south[p : p + 1, :] = plane[0:1, :]
            first = jnp.where(lane == p, plane[:, 0:1], first)
    east[...] = last
    west[...] = first


def split(x, pieces):
    out = []
    for i in range(pieces):
        top = x.astype(jnp.bfloat16)
        out.append(top)
        x = x - top.astype(jnp.float32)
    return out


def main_kernel(
    tr, es, ns, mix, om, fold, gat, from_south, from_north, from_west, from_east,
    cell, atm, owner, weight, out, table, total, mirror,
):
    tracer_count, level_count, row_count, cols = tr.shape
    lon_count = gat.shape[0]
    values = tracer_count + 1
    blocks = 1024 // LANES
    base = values * blocks
    hi_count = lon_count * blocks
    plane_count = tracer_count * level_count
    lat_count = lax.axis_size("lat")
    is_top = lax.axis_index("lat") == lat_count - 1

    coef = gat[:, tracer_count * blocks : base, :].reshape(hi_count, LANES)
    for t in range(values):
        if t < tracer_count:
            block = gat[:, t * blocks : (t + 1) * blocks, :].reshape(hi_count, LANES) * coef
        else:
            block = coef
        turned = block.T
        for i, piece in enumerate(split(turned, 2)):
            table[t * LANES : (t + 1) * LANES, i * hi_count : (i + 1) * hi_count] = piece

    total[...] = jnp.zeros_like(total)
    rows_each = WIDE // LANES

    def step(k, carry):
        def rows(ref):
            return jnp.concatenate(
                [ref[pl.ds(k * rows_each + i, 1), :] for i in range(rows_each)], axis=1
            )

        cells, atms, owners, weights = rows(cell), rows(atm), rows(owner), rows(weight)
        hi = owners * blocks + (atms >> 7)
        lo = atms & (LANES - 1)
        hi_hot = (lax.broadcasted_iota(jnp.int32, (hi_count, WIDE), 0) == hi).astype(
            jnp.float32
        ).astype(jnp.bfloat16)
        picked = jnp.dot(
            table[...], jnp.concatenate([hi_hot, hi_hot], axis=0),
            preferred_element_type=jnp.float32,
        )
        lane_row = lax.broadcasted_iota(jnp.int32, (LANES, WIDE), 0)
        lo_mask = lane_row == lo
        col_hot = (lane_row == (cells & (cols - 1))).astype(jnp.float32).astype(jnp.bfloat16)
        row_mask = lax.broadcasted_iota(jnp.int32, (row_count, WIDE), 0) == (cells >> 7)
        parts = []
        for t in range(values):
            chosen = jnp.where(lo_mask, picked[t * LANES : (t + 1) * LANES, :], 0.0)
            value = jnp.sum(chosen, axis=0, keepdims=True) * weights
            parts.append(jnp.where(row_mask, value, 0.0))
        left = jnp.concatenate(parts, axis=0)
        left = jnp.concatenate(split(left, 2), axis=0)
        total[...] += lax.dot_general(
            left, col_hot, (((1,), (1,)), ((), ())), preferred_element_type=jnp.float32
        )
        return carry

    lax.fori_loop(0, cell.shape[0] // rows_each, step, 0)

    mirror[...] = from_north[...]

    @pl.when(is_top)
    def _():
        lane_row = lax.broadcasted_iota(jnp.int32, (2 * LANES, LANES), 0)
        pad = mirror.shape[0]

        def fold_step(k, acc):
            both = jnp.concatenate(
                [gat[2 * k, base : base + pad, :], gat[2 * k + 1, base : base + pad, :]], axis=1
            )
            hot = (lane_row == fold[...] - k * (2 * LANES)).astype(jnp.float32).astype(jnp.bfloat16)
            return acc + jnp.dot(
                jnp.concatenate(split(both, 3), axis=0), hot, preferred_element_type=jnp.float32
            )

        acc = lax.fori_loop(
            0, lon_count // 2, fold_step, jnp.zeros((3 * pad, LANES), jnp.float32)
        )
        mirror[...] = acc[:pad] + acc[pad : 2 * pad] + acc[2 * pad :]

    mask = om[...].astype(jnp.float32)
    lane = lax.broadcasted_iota(jnp.int32, (row_count, cols), 1)
    row = lax.broadcasted_iota(jnp.int32, (row_count, cols), 0)
    west_cols = from_west[...]
    east_cols = from_east[...]

    def to_west(x, p):
        return jnp.where(lane == 0, west_cols[:, p : p + 1], pltpu.roll(x, 1, 1))

    def to_east(x, p):
        return jnp.where(lane == cols - 1, east_cols[:, p : p + 1], pltpu.roll(x, cols - 1, 1))

    def to_south(x, p):
        return jnp.where(row == 0, from_south[p : p + 1, :], pltpu.roll(x, 1, 0))

    def to_north(x, p):
        return jnp.where(row == row_count - 1, mirror[p : p + 1, :], pltpu.roll(x, row_count - 1, 0))

    mask_at = plane_count
    open_east = mask * to_east(mask, mask_at)
    open_west = to_west(mask, mask_at) * mask
    open_north = mask * to_north(mask, mask_at)
    open_south = to_south(mask, mask_at) * mask
    pivots = []
    ratios = []
    for level in range(level_count):
        lower = mix[level] if level < level_count - 1 else jnp.zeros_like(mask)
        if level == 0:
            pivot = 1.0 + lower
        else:
            pivot = 1.0 + mix[level - 1] + lower - mix[level - 1] * ratios[-1]
        inverse = 1.0 / pivot
        pivots.append(inverse)
        ratios.append(lower * inverse)
    done = [[] for _ in range(tracer_count)]
    lines = tracer_count + 1
    half = lines * row_count
    sums = total[0:half, :] + total[half : 2 * half, :]
    last_sum = sums[tracer_count * row_count :, :]
    for level in range(level_count):
        speed_e = es[level]
        speed_w = to_west(speed_e, mask_at + 1 + level)
        speed_n = ns[level]
        speed_s = to_south(speed_n, mask_at + 1 + level)
        for t in range(tracer_count):
            p = t * level_count + level
            x = tr[t, level]
            flux_e = speed_e * jnp.where(speed_e > 0, x, to_east(x, p)) * open_east
            flux_w = speed_w * jnp.where(speed_w > 0, to_west(x, p), x) * open_west
            flux_n = speed_n * jnp.where(speed_n > 0, x, to_north(x, p)) * open_north
            flux_s = speed_s * jnp.where(speed_s > 0, to_south(x, p), x) * open_south
            value = x - (flux_e - flux_w + flux_n - flux_s)
            if level == 0:
                surface = sums[t * row_count : (t + 1) * row_count, :] - x * last_sum
                value = value + flux_step * surface
            else:
                value = value + mix[level - 1] * done[t][-1]
            done[t].append(value * pivots[level])
    for t in range(tracer_count):
        x = done[t][-1]
        out[t, level_count - 1] = x * mask
        for level in range(level_count - 2, -1, -1):
            x = done[t][level] + ratios[level] * x
            out[t, level] = x * mask


def body(
    tracers,
    east_speed,
    north_speed,
    mixing_coef,
    ocean_mask,
    fold_map,
    atmos_state,
    atmos_coef,
    xgrid_cell,
    xgrid_atm,
    xgrid_owner,
    xgrid_weight,
):
    tracer_count, level_count, row_count, cols = tracers.shape
    lon_count = lax.axis_size("lon")
    lat_count = lax.axis_size("lat")
    plane_count = tracer_count * level_count
    blocks = atmos_coef.shape[0] // LANES
    base = (tracer_count + 1) * blocks
    pad = -(-(plane_count + 1) // 8) * 8
    north_pad = -(-(plane_count + 1 + level_count) // 8) * 8
    f32 = jnp.float32
    vmem = pl.BlockSpec(memory_space=pltpu.VMEM)
    gat, north, south, east, west = pl.pallas_call(
        pack_kernel,
        out_shape=(
            jax.ShapeDtypeStruct((base + pad, cols), f32),
            jax.ShapeDtypeStruct((north_pad, cols), f32),
            jax.ShapeDtypeStruct((pad, cols), f32),
            jax.ShapeDtypeStruct((row_count, cols), f32),
            jax.ShapeDtypeStruct((row_count, cols), f32),
        ),
        in_specs=[vmem] * 6,
        out_specs=(vmem,) * 5,
        name="pack_edges",
    )(tracers, east_speed, north_speed, ocean_mask, atmos_state, atmos_coef.reshape(blocks, LANES))
    gathered = lax.all_gather(gat, "lon", axis=0, tiled=False)
    up_lat = [(i, i + 1) for i in range(lat_count - 1)]
    down_lat = [(j, i) for i, j in up_lat]
    up_lon = [(i, (i + 1) % lon_count) for i in range(lon_count)]
    down_lon = [(j, i) for i, j in up_lon]
    from_south = lax.ppermute(north, "lat", up_lat)
    from_north = lax.ppermute(south, "lat", down_lat)
    from_west = lax.ppermute(east, "lon", up_lon)
    from_east = lax.ppermute(west, "lon", down_lon)
    rows = xgrid_cell.shape[0] // LANES
    return pl.pallas_call(
        main_kernel,
        out_shape=jax.ShapeDtypeStruct(tracers.shape, f32),
        in_specs=[vmem] * 15,
        out_specs=vmem,
        scratch_shapes=[
            pltpu.VMEM(((tracer_count + 1) * LANES, 2 * lon_count * blocks), jnp.bfloat16),
            pltpu.VMEM((2 * (tracer_count + 1) * row_count, cols), f32),
            pltpu.VMEM((pad, cols), f32),
        ],
        name="exchange_and_solve",
    )(
        tracers, east_speed, north_speed, mixing_coef, ocean_mask, fold_map.reshape(1, cols),
        gathered, from_south, from_north, from_west, from_east,
        xgrid_cell.reshape(rows, LANES), xgrid_atm.reshape(rows, LANES),
        xgrid_owner.reshape(rows, LANES), xgrid_weight.reshape(rows, LANES),
    )


def solution(mesh):
    in_specs = (
        P(None, None, "lat", "lon"),
        P(None, "lat", "lon"),
        P(None, "lat", "lon"),
        P(None, "lat", "lon"),
        P("lat", "lon"),
        P("lon"),
        P(None, ("lon", "lat")),
        P(("lon", "lat")),
        P(("lon", "lat")),
        P(("lon", "lat")),
        P(("lon", "lat"), None),
        P(("lon", "lat")),
    )
    out_specs = P(None, None, "lat", "lon")
    return jax.shard_map(body, mesh=mesh, in_specs=in_specs, out_specs=out_specs, check_vma=False)
```

profile of v0, /device:TPU:16, one launch (start us, length us, event | category | flops | bytes accessed | tf_op | source)
XLA Modules:
  0.0 158.3 jit_solution(2782739862889266689)
XLA Ops:
  6.5 0.0 all-gather.3.cloned.1.call-start
  6.5 1.9 %pack_edges.1 = (f32[80,128]{1,0:T(8,128)}, f32[48,128]{1,0:T(8,128)}, f32[40,128]{1,0:T(8,128)}, f32[16,128]{1,0:T(8,128)}, f32[16,128]{1,0:T(8,128)}) custom-call(f32[4,8,16,128]{3,2,1,0:T(8,128)} %tr.3, f32[8,16,128]{2,1,0:T(8,128)} %es.3, f32[8,16,128]{2,1,0:T(8,128)} %ns.3, s32[16,128]{1,0:T(8,128)} %om.3, f32[4,1024]{1,0:T(4,128)} %state.1, ...), custom_call_target="tpu_custom_call" | custom-call | tf_op jit(solution)/shard_map/pack_edges/pallas_call | solution.py:230
  8.4 0.0 all-gather.3.cloned.1.call-update
  8.5 1.7 %collective-permute-start = (f32[48,128]{1,0:T(8,128)}, f32[48,128]{1,0:T(8,128)S(1)}, u32[]{:S(2)}, u32[]{:S(2)}) collective-permute-start(f32[48,128]{1,0:T(8,128)} %get-tuple-element.11), channel_id=1, source_target_pairs={{0,1},{1,2},{2,3},{3,4},{4,5},{5,6},{6,7},{7,8},{8,9},{9,10},{10,1... | collective-permute-start | bytes 73736 | tf_op jit(solution)/shard_map/ppermute | solution.py:248
  10.2 1.3 collective-permute-start.1
  11.5 4.3 %collective-permute-start.2 = (f32[16,128]{1,0:T(8,128)}, f32[16,128]{1,0:T(8,128)S(1)}, u32[]{:S(2)}, u32[]{:S(2)}) collective-permute-start(f32[16,128]{1,0:T(8,128)} %get-tuple-element.13), channel_id=1, source_target_pairs={{0,16},{16,32},{32,48},{48,64},{64,80},{80,96},{96,112},{112,128},... | collective-permute-start | bytes 24584 | tf_op jit(solution)/shard_map/ppermute | solution.py:250
  15.8 12.0 %collective-permute-start.3 = (f32[16,128]{1,0:T(8,128)}, f32[16,128]{1,0:T(8,128)S(1)}, u32[]{:S(2)}, u32[]{:S(2)}) collective-permute-start(f32[16,128]{1,0:T(8,128)} %get-tuple-element.14), channel_id=1, source_target_pairs={{16,0},{32,16},{48,32},{64,48},{80,64},{96,80},{112,96},{128,112},... | collective-permute-start | bytes 24584 | tf_op jit(solution)/shard_map/ppermute | solution.py:251
  27.8 0.0 collective-permute-done.2.from_west
  27.8 0.0 copy-start.2
  27.8 1.5 collective-permute-done.3.from_east
  29.4 0.0 copy-start.3
  29.4 0.0 collective-permute-done.1.from_north
  29.4 0.0 copy-start.1
  29.4 0.0 collective-permute-done.from_south
  29.4 0.0 copy-start
  29.4 107.9 %all-gather.3.cloned.1.call-done = f32[3840,128]{1,0:T(8,128)} async-done(((f32[80,128]{1,0:T(8,128)}), f32[3840,128]{1,0:T(8,128)}) %all-gather.3.cloned.1.call-update) | async-done | bytes 1966096 | tf_op jit(solution)/shard_map/all_gather | solution.py:243
  137.3 0.0 copy-done.2
  137.3 0.0 copy-done.3
  137.3 0.0 copy-done.1
  137.3 0.0 copy-done
  137.3 14.1 %exchange_and_solve.1 = f32[4,8,16,128]{3,2,1,0:T(8,128)} custom-call(f32[4,8,16,128]{3,2,1,0:T(8,128)} %tr.3, f32[8,16,128]{2,1,0:T(8,128)} %es.3, f32[8,16,128]{2,1,0:T(8,128)} %ns.3, f32[7,16,128]{2,1,0:T(8,128)} %mix.1, s32[16,128]{1,0:T(8,128)} %om.3, s32[1,128]{1,0:T(1,128)} %bitcast.13, f32[48,80,128]{2,1,0:T(8,128)} %bitcast.7, f32[48,128]{1,0:T(8,128)} %copy-done, ...), custom_call_target="tpu_custom_call" | custom-call | tf_op jit(solution)/shard_map/exchange_and_solve/pallas_call | solution.py:253
Async XLA Ops:
  6.5 130.8 %all-gather.3.cloned.1.call-start = ((), (), s32[]{:S(2)}) async-start(), calls=%async_computation | async-start | bytes 2007040 | tf_op jit(solution)/shard_map/all_gather | solution.py:243
  8.5 20.9 %collective-permute-start = (f32[48,128]{1,0:T(8,128)}, f32[48,128]{1,0:T(8,128)S(1)}, u32[]{:S(2)}, u32[]{:S(2)}) collective-permute-start(f32[48,128]{1,0:T(8,128)} %get-tuple-element.11), channel_id=1, source_target_pairs={{0,1},{1,2},{2,3},{3,4},{4,5},{5,6},{6,7},{7,8},{8,9},{9,10},{10,1... | collective-permute-start | bytes 73736 | tf_op jit(solution)/shard_map/ppermute | solution.py:248
  10.2 19.2 %collective-permute-start.1 = (f32[40,128]{1,0:T(8,128)}, f32[40,128]{1,0:T(8,128)S(1)}, u32[]{:S(2)}, u32[]{:S(2)}) collective-permute-start(f32[40,128]{1,0:T(8,128)} %get-tuple-element.12), channel_id=1, source_target_pairs={{1,0},{2,1},{3,2},{4,3},{5,4},{6,5},{7,6},{8,7},{9,8},{10,9},{11,1... | collective-permute-start | bytes 61448 | tf_op jit(solution)/shard_map/ppermute | solution.py:249
  11.5 16.3 %collective-permute-start.2 = (f32[16,128]{1,0:T(8,128)}, f32[16,128]{1,0:T(8,128)S(1)}, u32[]{:S(2)}, u32[]{:S(2)}) collective-permute-start(f32[16,128]{1,0:T(8,128)} %get-tuple-element.13), channel_id=1, source_target_pairs={{0,16},{16,32},{32,48},{48,64},{64,80},{80,96},{96,112},{112,128},... | collective-permute-start | bytes 24584 | tf_op jit(solution)/shard_map/ppermute | solution.py:250
  15.8 13.6 %collective-permute-start.3 = (f32[16,128]{1,0:T(8,128)}, f32[16,128]{1,0:T(8,128)S(1)}, u32[]{:S(2)}, u32[]{:S(2)}) collective-permute-start(f32[16,128]{1,0:T(8,128)} %get-tuple-element.14), channel_id=1, source_target_pairs={{16,0},{32,16},{48,32},{64,48},{80,64},{96,80},{112,96},{128,112},... | collective-permute-start | bytes 24584 | tf_op jit(solution)/shard_map/ppermute | solution.py:251
  27.8 109.5 %copy-start.2 = (f32[16,128]{1,0:T(8,128)}, f32[16,128]{1,0:T(8,128)S(1)}, u32[]{:S(2)}) copy-start(f32[16,128]{1,0:T(8,128)S(1)} %collective-permute-done.2.from_west) | copy-start | bytes 24580
  29.4 108.0 %copy-start.3 = (f32[16,128]{1,0:T(8,128)}, f32[16,128]{1,0:T(8,128)S(1)}, u32[]{:S(2)}) copy-start(f32[16,128]{1,0:T(8,128)S(1)} %collective-permute-done.3.from_east) | copy-start | bytes 24580
  29.4 108.0 %copy-start.1 = (f32[40,128]{1,0:T(8,128)}, f32[40,128]{1,0:T(8,128)S(1)}, u32[]{:S(2)}) copy-start(f32[40,128]{1,0:T(8,128)S(1)} %collective-permute-done.1.from_north) | copy-start | bytes 61444
  29.4 108.0 %copy-start = (f32[48,128]{1,0:T(8,128)}, f32[48,128]{1,0:T(8,128)S(1)}, u32[]{:S(2)}) copy-start(f32[48,128]{1,0:T(8,128)S(1)} %collective-permute-done.from_south) | copy-start | bytes 73732
Sparse Core Ops, SparseCore 0:
  11.0 126.2 all-gather.2
where the time goes:
time: 158 us
  waiting for transfers between devices  110 us (70%)
  starting transfers between devices  19.3 us (12%)
  Pallas kernels  16 us (10%)
  between operations  13.5 us (9%)
    all_gather x1, waiting for transfers between devices, body(): gathered = lax.all_gather(gat, 'lon', axis=0, tiled=False)  108 us
    pallas_call x1, Pallas kernels, body(): pl.pallas_call(main_kernel, out_shape=jax.ShapeDtypeStruct(tracers.shape,...  14.1 us
    ppermute x1, starting transfers between devices, body(): from_east = lax.ppermute(west, 'lon', down_lon)  12 us
    ppermute x1, starting transfers between devices, body(): from_west = lax.ppermute(east, 'lon', up_lon)  4.28 us
  transfers between devices with their start and end apart: 5, of which 2 were waited for; matrix products, arithmetic and copies ran while one was open for 0% of the time, Pallas kernels for 0%

commit v1 on v0

--- a/solution.py
+++ b/solution.py
@@ -8,20 +8,19 @@
 flux_step = 0.5
 LANES = 128
 WIDE = 512
-
-
-def pack_kernel(tr, es, ns, om, state, coef, gat, north, south, east, west):
+Y_GROUPS = 4
+
+
+def pack_kernel(tr, es, ns, om, state, coef, air, north, south, east, west):
     tracer_count, level_count, row_count, cols = tr.shape
     blocks = state.shape[1] // LANES
     for t in range(tracer_count):
         for h in range(blocks):
-            gat[t * blocks + h : t * blocks + h + 1, :] = state[t : t + 1, h * LANES : (h + 1) * LANES]
-    gat[tracer_count * blocks : (tracer_count + 1) * blocks, :] = coef[...]
-    base = (tracer_count + 1) * blocks
+            air[t * blocks + h : t * blocks + h + 1, :] = state[t : t + 1, h * LANES : (h + 1) * LANES]
+    air[tracer_count * blocks : (tracer_count + 1) * blocks, :] = coef[...]
     plane_count = tracer_count * level_count
     lane = lax.broadcasted_iota(jnp.int32, (row_count, cols), 1)
     mask = om[...].astype(jnp.float32)
-    gat[base:, :] = jnp.zeros((gat.shape[0] - base, cols), jnp.float32)
     north[...] = jnp.zeros_like(north)
     south[...] = jnp.zeros_like(south)
     first = jnp.zeros((row_count, cols), jnp.float32)
@@ -39,11 +38,135 @@
         north[p : p + 1, :] = north_plane[row_count - 1 : row_count, :]
         last = jnp.where(lane == p, plane[:, cols - 1 : cols], last)
         if p <= plane_count:
-            gat[base + p : base + p + 1, :] = plane[row_count - 1 : row_count, :]
             south[p : p + 1, :] = plane[0:1, :]
             first = jnp.where(lane == p, plane[:, 0:1], first)
     east[...] = last
     west[...] = first
+
+
+def exchange_kernel(
+    air, north, south, east, west,
+    air_all, top_all, from_south, from_north, from_west, from_east,
+    send_air, recv_air, send_top, recv_top, send_edge, recv_edge, own,
+):
+    z_count = air_all.shape[0]
+    lon_count = z_count * Y_GROUPS
+    lat_count = lax.axis_size("lat")
+    lon = lax.axis_index("lon")
+    lat = lax.axis_index("lat")
+    z = lax.rem(lon, z_count)
+    y_base = lon - z
+    z_right = {"lon": y_base + lax.rem(z + 1, z_count)}
+    z_left = {"lon": y_base + lax.rem(z + z_count - 1, z_count)}
+    y_to = [{"lon": lax.rem(lon + d * z_count, lon_count)} for d in range(Y_GROUPS)]
+    lon_right = {"lon": lax.rem(lon + 1, lon_count)}
+    lon_left = {"lon": lax.rem(lon + lon_count - 1, lon_count)}
+    lat_up = {"lat": lax.rem(lat + 1, lat_count)}
+    lat_down = {"lat": lax.rem(lat + lat_count - 1, lat_count)}
+    partners = [z_right, z_left, lon_right, lon_left, lat_up, lat_down] + y_to[1:]
+    is_top = lat == lat_count - 1
+    mesh_ids = pl.DeviceIdType.MESH
+
+    barrier = pltpu.get_barrier_semaphore()
+    for partner in partners:
+        pl.semaphore_signal(barrier, inc=1, device_id=partner, device_id_type=mesh_ids)
+    pl.semaphore_wait(barrier, len(partners))
+
+    edges = []
+    for i, (src, dst, target) in enumerate(
+        ((north, from_south, lat_up), (south, from_north, lat_down),
+         (east, from_west, lon_right), (west, from_east, lon_left))
+    ):
+        edges.append(
+            pltpu.make_async_remote_copy(
+                src_ref=src, dst_ref=dst, send_sem=send_edge.at[i], recv_sem=recv_edge.at[i],
+                device_id=target, device_id_type=mesh_ids,
+            )
+        )
+
+    right_steps = z_count // 2
+    left_steps = z_count - 1 - right_steps
+    pad = top_all.shape[2]
+
+    def flow(first, slots, send, recv):
+        def copy(slot, d):
+            if slot == 0:
+                src, target = first, y_to[d]
+            elif slot <= right_steps:
+                before = slot - 1
+                src = first if before == 0 and d == 0 else slots.at[before, d]
+                target = z_right
+            else:
+                before = (slot + 1) % z_count
+                src = first if before == 0 and d == 0 else slots.at[before, d]
+                target = z_left
+            return pltpu.make_async_remote_copy(
+                src_ref=src, dst_ref=slots.at[slot, d], send_sem=send.at[slot, d],
+                recv_sem=recv.at[slot, d], device_id=target, device_id_type=mesh_ids,
+            )
+
+        return copy
+
+    air_flow = flow(air, air_all, send_air, recv_air)
+    top_flow = flow(north.at[0:pad], top_all, send_top, recv_top)
+    air_own = pltpu.make_async_copy(air, air_all.at[0, 0], own.at[0])
+    top_own = pltpu.make_async_copy(north.at[0:pad], top_all.at[0, 0], own.at[1])
+
+    def begin(copy):
+        for d in range(1, Y_GROUPS):
+            copy(0, d).start()
+        copy(1, 0).start()
+        copy(z_count - 1, 0).start()
+
+    def advance(copy, step):
+        for d in range(Y_GROUPS):
+            if step == 0:
+                if d > 0:
+                    copy(0, d).wait_recv()
+                    copy(1, d).start()
+                    copy(z_count - 1, d).start()
+                continue
+            copy(step, d).wait_recv()
+            if step < right_steps:
+                copy(step + 1, d).start()
+            if step <= left_steps:
+                copy(z_count - step, d).wait_recv()
+                if step < left_steps:
+                    copy(z_count - step - 1, d).start()
+
+    def finish(copy):
+        for slot in range(z_count):
+            for d in range(Y_GROUPS):
+                if slot or d:
+                    copy(slot, d).wait_send()
+
+    for edge in edges:
+        edge.start()
+    begin(air_flow)
+    air_own.start()
+
+    @pl.when(is_top)
+    def _():
+        begin(top_flow)
+        top_own.start()
+
+    for step in range(right_steps + 1):
+        advance(air_flow, step)
+
+        @pl.when(is_top)
+        def _():
+            advance(top_flow, step)
+
+    finish(air_flow)
+    air_own.wait()
+
+    @pl.when(is_top)
+    def _():
+        finish(top_flow)
+        top_own.wait()
+
+    for edge in edges:
+        edge.wait()
 
 
 def split(x, pieces):
@@ -56,7 +179,7 @@
 
 
 def main_kernel(
-    tr, es, ns, mix, om, fold, gat, from_south, from_north, from_west, from_east,
+    tr, es, ns, mix, om, fold, gat, top_rows, from_south, from_north, from_west, from_east,
     cell, atm, owner, weight, out, table, total, mirror,
 ):
     tracer_count, level_count, row_count, cols = tr.shape
@@ -65,9 +188,24 @@
     blocks = 1024 // LANES
     base = values * blocks
     hi_count = lon_count * blocks
+    z_count = lon_count // Y_GROUPS
+    lon = lax.axis_index("lon")
+    my_z = lax.rem(lon, z_count)
+    my_y = lax.div(lon, z_count)
     plane_count = tracer_count * level_count
     lat_count = lax.axis_size("lat")
     is_top = lax.axis_index("lat") == lat_count - 1
+    is_bottom = lax.axis_index("lat") == 0
+
+    def place_of(owners):
+        y = jnp.zeros_like(owners)
+        for group in range(1, Y_GROUPS):
+            y = y + (owners >= group * z_count).astype(jnp.int32)
+        far_z = my_z - (owners - y * z_count)
+        far_y = my_y - y
+        far_z = jnp.where(far_z < 0, far_z + z_count, far_z)
+        far_y = jnp.where(far_y < 0, far_y + Y_GROUPS, far_y)
+        return far_z * Y_GROUPS + far_y
 
     coef = gat[:, tracer_count * blocks : base, :].reshape(hi_count, LANES)
     for t in range(values):
@@ -89,7 +227,7 @@
             )
 
         cells, atms, owners, weights = rows(cell), rows(atm), rows(owner), rows(weight)
-        hi = owners * blocks + (atms >> 7)
+        hi = place_of(owners) * blocks + (atms >> 7)
         lo = atms & (LANES - 1)
         hi_hot = (lax.broadcasted_iota(jnp.int32, (hi_count, WIDE), 0) == hi).astype(
             jnp.float32
@@ -122,12 +260,13 @@
     def _():
         lane_row = lax.broadcasted_iota(jnp.int32, (2 * LANES, LANES), 0)
         pad = mirror.shape[0]
+        spot = place_of(fold[...] >> 7) * LANES + (fold[...] & (LANES - 1))
 
         def fold_step(k, acc):
             both = jnp.concatenate(
-                [gat[2 * k, base : base + pad, :], gat[2 * k + 1, base : base + pad, :]], axis=1
+                [top_rows[2 * k], top_rows[2 * k + 1]], axis=1
             )
-            hot = (lane_row == fold[...] - k * (2 * LANES)).astype(jnp.float32).astype(jnp.bfloat16)
+            hot = (lane_row == spot - k * (2 * LANES)).astype(jnp.float32).astype(jnp.bfloat16)
             return acc + jnp.dot(
                 jnp.concatenate(split(both, 3), axis=0), hot, preferred_element_type=jnp.float32
             )
@@ -142,6 +281,7 @@
     row = lax.broadcasted_iota(jnp.int32, (row_count, cols), 0)
     west_cols = from_west[...]
     east_cols = from_east[...]
+    south_rows = jnp.where(is_bottom, 0.0, from_south[...])
 
     def to_west(x, p):
         return jnp.where(lane == 0, west_cols[:, p : p + 1], pltpu.roll(x, 1, 1))
@@ -150,7 +290,7 @@
         return jnp.where(lane == cols - 1, east_cols[:, p : p + 1], pltpu.roll(x, cols - 1, 1))
 
     def to_south(x, p):
-        return jnp.where(row == 0, from_south[p : p + 1, :], pltpu.roll(x, 1, 0))
+        return jnp.where(row == 0, south_rows[p : p + 1, :], pltpu.roll(x, 1, 0))
 
     def to_north(x, p):
         return jnp.where(row == row_count - 1, mirror[p : p + 1, :], pltpu.roll(x, row_count - 1, 0))
@@ -227,33 +367,46 @@
     north_pad = -(-(plane_count + 1 + level_count) // 8) * 8
     f32 = jnp.float32
     vmem = pl.BlockSpec(memory_space=pltpu.VMEM)
-    gat, north, south, east, west = pl.pallas_call(
+    edges = (
+        jax.ShapeDtypeStruct((north_pad, cols), f32),
+        jax.ShapeDtypeStruct((pad, cols), f32),
+        jax.ShapeDtypeStruct((row_count, cols), f32),
+        jax.ShapeDtypeStruct((row_count, cols), f32),
+    )
+    air, north, south, east, west = pl.pallas_call(
         pack_kernel,
-        out_shape=(
-            jax.ShapeDtypeStruct((base + pad, cols), f32),
-            jax.ShapeDtypeStruct((north_pad, cols), f32),
-            jax.ShapeDtypeStruct((pad, cols), f32),
-            jax.ShapeDtypeStruct((row_count, cols), f32),
-            jax.ShapeDtypeStruct((row_count, cols), f32),
-        ),
+        out_shape=(jax.ShapeDtypeStruct((base, cols), f32),) + edges,
         in_specs=[vmem] * 6,
         out_specs=(vmem,) * 5,
         name="pack_edges",
     )(tracers, east_speed, north_speed, ocean_mask, atmos_state, atmos_coef.reshape(blocks, LANES))
-    gathered = lax.all_gather(gat, "lon", axis=0, tiled=False)
-    up_lat = [(i, i + 1) for i in range(lat_count - 1)]
-    down_lat = [(j, i) for i, j in up_lat]
-    up_lon = [(i, (i + 1) % lon_count) for i in range(lon_count)]
-    down_lon = [(j, i) for i, j in up_lon]
-    from_south = lax.ppermute(north, "lat", up_lat)
-    from_north = lax.ppermute(south, "lat", down_lat)
-    from_west = lax.ppermute(east, "lon", up_lon)
-    from_east = lax.ppermute(west, "lon", down_lon)
+    z_count = lon_count // Y_GROUPS
+    spots = (z_count, Y_GROUPS)
+    air_all, top_all, from_south, from_north, from_west, from_east = pl.pallas_call(
+        exchange_kernel,
+        out_shape=(
+            jax.ShapeDtypeStruct(spots + (base, cols), f32),
+            jax.ShapeDtypeStruct(spots + (pad, cols), f32),
+        ) + edges,
+        in_specs=[vmem] * 5,
+        out_specs=(vmem,) * 6,
+        scratch_shapes=[
+            pltpu.SemaphoreType.DMA(spots),
+            pltpu.SemaphoreType.DMA(spots),
+            pltpu.SemaphoreType.DMA(spots),
+            pltpu.SemaphoreType.DMA(spots),
+            pltpu.SemaphoreType.DMA((4,)),
+            pltpu.SemaphoreType.DMA((4,)),
+            pltpu.SemaphoreType.DMA((2,)),
+        ],
+        compiler_params=pltpu.CompilerParams(collective_id=0, has_side_effects=True),
+        name="exchange_edges",
+    )(air, north, south, east, west)
     rows = xgrid_cell.shape[0] // LANES
     return pl.pallas_call(
         main_kernel,
         out_shape=jax.ShapeDtypeStruct(tracers.shape, f32),
-        in_specs=[vmem] * 15,
+        in_specs=[vmem] * 16,
         out_specs=vmem,
         scratch_shapes=[
             pltpu.VMEM(((tracer_count + 1) * LANES, 2 * lon_count * blocks), jnp.bfloat16),
@@ -263,7 +416,7 @@
         name="exchange_and_solve",
     )(
         tracers, east_speed, north_speed, mixing_coef, ocean_mask, fold_map.reshape(1, cols),
-        gathered, from_south, from_north, from_west, from_east,
+        air_all.reshape(lon_count, base, cols), top_all.reshape(lon_count, pad, cols), from_south, from_north, from_west, from_east,
         xgrid_cell.reshape(rows, LANES), xgrid_atm.reshape(rows, LANES),
         xgrid_owner.reshape(rows, LANES), xgrid_weight.reshape(rows, LANES),
     )

time: 158 us -> 62.3 us (0.39)
  the two profiles are of different devices: /device:TPU:16 before, /device:TPU:15 now
where the time goes in v1:
time: 62.3 us; the launch traced here: 62 us
  Pallas kernels  62 us (100%)
    pallas_call x1, Pallas kernels, body(): pl.pallas_call(exchange_kernel, out_shape=(jax.ShapeDtypeStruct(spots + (...  42.3 us
    pallas_call x1, Pallas kernels, body(): pl.pallas_call(main_kernel, out_shape=jax.ShapeDtypeStruct(tracers.shape,...  17.8 us
    pallas_call x1, Pallas kernels, body(): pl.pallas_call(pack_kernel, out_shape=(jax.ShapeDtypeStruct((base, cols),...  1.89 us

profile of v1, /device:TPU:15, one launch (start us, length us, event | category | flops | bytes accessed | tf_op | source)
XLA Modules:
  0.0 62.0 jit_solution(2810167956867453541)
XLA Ops:
  0.0 1.9 %pack_edges.1 = (f32[40,128]{1,0:T(8,128)}, f32[48,128]{1,0:T(8,128)}, f32[40,128]{1,0:T(8,128)}, f32[16,128]{1,0:T(8,128)}, f32[16,128]{1,0:T(8,128)}) custom-call(f32[4,8,16,128]{3,2,1,0:T(8,128)} %tr.3, f32[8,16,128]{2,1,0:T(8,128)} %es.3, f32[8,16,128]{2,1,0:T(8,128)} %ns.3, s32[16,128]{1,0:T(8,128)} %om.3, f32[4,1024]{1,0:T(4,128)} %state.1, ...), custom_call_target="tpu_custom_call" | custom-call | tf_op jit(solution)/shard_map/pack_edges/pallas_call | solution.py:376
  1.9 42.3 %exchange_edges.1 = (f32[12,4,40,128]{3,2,1,0:T(8,128)}, f32[12,4,40,128]{3,2,1,0:T(8,128)}, f32[48,128]{1,0:T(8,128)}, f32[40,128]{1,0:T(8,128)}, f32[16,128]{1,0:T(8,128)}, /*index=5*/f32[16,128]{1,0:T(8,128)}) custom-call(f32[40,128]{1,0:T(8,128)} %get-tuple-element.16.air, f32[48,128]{1,0:T(8,128)} %get-tuple-element.17.north, ...), custom_call_target="tpu_custom_call" | custom-call | tf_op jit(solution)/shard_map/exchange_edges/pallas_call | solution.py:385
  44.2 17.8 %exchange_and_solve.1 = f32[4,8,16,128]{3,2,1,0:T(8,128)} custom-call(f32[4,8,16,128]{3,2,1,0:T(8,128)} %tr.3, f32[8,16,128]{2,1,0:T(8,128)} %es.3, f32[8,16,128]{2,1,0:T(8,128)} %ns.3, f32[7,16,128]{2,1,0:T(8,128)} %mix.1, s32[16,128]{1,0:T(8,128)} %om.3, s32[1,128]{1,0:T(1,128)} %bitcast.15, f32[48,40,128]{2,1,0:T(8,128)} %bitcast.8, ...), custom_call_target="tpu_custom_call" | custom-call | tf_op jit(solution)/shard_map/exchange_and_solve/pallas_call | solution.py:406

commit v2 on v1

--- a/solution.py
+++ b/solution.py
@@ -7,7 +7,8 @@
 
 flux_step = 0.5
 LANES = 128
-WIDE = 512
+WIDE = 2048
+FOLD_STEP = 16
 Y_GROUPS = 4
 
 
@@ -118,21 +119,28 @@
         copy(1, 0).start()
         copy(z_count - 1, 0).start()
 
-    def advance(copy, step):
-        for d in range(Y_GROUPS):
-            if step == 0:
-                if d > 0:
-                    copy(0, d).wait_recv()
-                    copy(1, d).start()
-                    copy(z_count - 1, d).start()
-                continue
-            copy(step, d).wait_recv()
-            if step < right_steps:
-                copy(step + 1, d).start()
-            if step <= left_steps:
-                copy(z_count - step, d).wait_recv()
-                if step < left_steps:
-                    copy(z_count - step - 1, d).start()
+    def advance(copy, step, d):
+        if step == 0:
+            if d > 0:
+                copy(0, d).wait_recv()
+                copy(1, d).start()
+                copy(z_count - 1, d).start()
+            return
+        copy(step, d).wait_recv()
+        if step < right_steps:
+            copy(step + 1, d).start()
+        if step <= left_steps:
+            copy(z_count - step, d).wait_recv()
+            if step < left_steps:
+                copy(z_count - step - 1, d).start()
+
+    order = []
+    for d in range(Y_GROUPS):
+        delay = 0.5 + 0.7 * min(d, Y_GROUPS - d) if d else 0.0
+        for step in range(right_steps + 1):
+            order.append((step + delay, d, step, False))
+            order.append((step + delay + 0.6, d, step, True))
+    order.sort()
 
     def finish(copy):
         for slot in range(z_count):
@@ -150,12 +158,15 @@
         begin(top_flow)
         top_own.start()
 
-    for step in range(right_steps + 1):
-        advance(air_flow, step)
-
-        @pl.when(is_top)
-        def _():
-            advance(top_flow, step)
+    for _, d, step, is_fold in order:
+        if is_fold:
+
+            @pl.when(is_top)
+            def _():
+                advance(top_flow, step, d)
+
+        else:
+            advance(air_flow, step, d)
 
     finish(air_flow)
     air_own.wait()
@@ -258,23 +269,24 @@
 
     @pl.when(is_top)
     def _():
-        lane_row = lax.broadcasted_iota(jnp.int32, (2 * LANES, LANES), 0)
+        depth = FOLD_STEP * LANES
+        lane_row = lax.broadcasted_iota(jnp.int32, (depth, LANES), 0)
         pad = mirror.shape[0]
         spot = place_of(fold[...] >> 7) * LANES + (fold[...] & (LANES - 1))
 
         def fold_step(k, acc):
-            both = jnp.concatenate(
-                [top_rows[2 * k], top_rows[2 * k + 1]], axis=1
+            block = jnp.concatenate(
+                [top_rows[FOLD_STEP * k + i] for i in range(FOLD_STEP)], axis=1
             )
-            hot = (lane_row == spot - k * (2 * LANES)).astype(jnp.float32).astype(jnp.bfloat16)
+            hot = (lane_row == spot - k * depth).astype(jnp.float32).astype(jnp.bfloat16)
             return acc + jnp.dot(
-                jnp.concatenate(split(both, 3), axis=0), hot, preferred_element_type=jnp.float32
+                jnp.concatenate(split(block, 2), axis=0), hot, preferred_element_type=jnp.float32
             )
 
         acc = lax.fori_loop(
-            0, lon_count // 2, fold_step, jnp.zeros((3 * pad, LANES), jnp.float32)
+            0, lon_count // FOLD_STEP, fold_step, jnp.zeros((2 * pad, LANES), jnp.float32)
         )
-        mirror[...] = acc[:pad] + acc[pad : 2 * pad] + acc[2 * pad :]
+        mirror[...] = acc[:pad] + acc[pad:]
 
     mask = om[...].astype(jnp.float32)
     lane = lax.broadcasted_iota(jnp.int32, (row_count, cols), 1)

time: 62.3 us -> 59.4 us (0.953)
  the two profiles are of different devices: /device:TPU:15 before, /device:TPU:6 now
where the time goes in v2:
time: 59.4 us; the launch traced here: 59.2 us
  Pallas kernels  59.2 us (100%)
    pallas_call x1, Pallas kernels, body(): pl.pallas_call(exchange_kernel, out_shape=(jax.ShapeDtypeStruct(spots + (...  45.7 us
    pallas_call x1, Pallas kernels, body(): pl.pallas_call(main_kernel, out_shape=jax.ShapeDtypeStruct(tracers.shape,...  11.5 us
    pallas_call x1, Pallas kernels, body(): pl.pallas_call(pack_kernel, out_shape=(jax.ShapeDtypeStruct((base, cols),...  1.89 us

profile of v2, /device:TPU:6, one launch (start us, length us, event | category | flops | bytes accessed | tf_op | source)
XLA Modules:
  0.0 59.2 jit_solution(10475651791754951155)
XLA Ops:
  0.0 1.9 %pack_edges.1 = (f32[40,128]{1,0:T(8,128)}, f32[48,128]{1,0:T(8,128)}, f32[40,128]{1,0:T(8,128)}, f32[16,128]{1,0:T(8,128)}, f32[16,128]{1,0:T(8,128)}) custom-call(f32[4,8,16,128]{3,2,1,0:T(8,128)} %tr.3, f32[8,16,128]{2,1,0:T(8,128)} %es.3, f32[8,16,128]{2,1,0:T(8,128)} %ns.3, s32[16,128]{1,0:T(8,128)} %om.3, f32[4,1024]{1,0:T(4,128)} %state.1, ...), custom_call_target="tpu_custom_call" | custom-call | tf_op jit(solution)/shard_map/pack_edges/pallas_call | solution.py:388
  1.9 45.7 %exchange_edges.1 = (f32[12,4,40,128]{3,2,1,0:T(8,128)}, f32[12,4,40,128]{3,2,1,0:T(8,128)}, f32[48,128]{1,0:T(8,128)}, f32[40,128]{1,0:T(8,128)}, f32[16,128]{1,0:T(8,128)}, /*index=5*/f32[16,128]{1,0:T(8,128)}) custom-call(f32[40,128]{1,0:T(8,128)} %get-tuple-element.16.air, f32[48,128]{1,0:T(8,128)} %get-tuple-element.17.north, ...), custom_call_target="tpu_custom_call" | custom-call | tf_op jit(solution)/shard_map/exchange_edges/pallas_call | solution.py:397
  47.6 11.5 %exchange_and_solve.1 = f32[4,8,16,128]{3,2,1,0:T(8,128)} custom-call(f32[4,8,16,128]{3,2,1,0:T(8,128)} %tr.3, f32[8,16,128]{2,1,0:T(8,128)} %es.3, f32[8,16,128]{2,1,0:T(8,128)} %ns.3, f32[7,16,128]{2,1,0:T(8,128)} %mix.1, s32[16,128]{1,0:T(8,128)} %om.3, s32[1,128]{1,0:T(1,128)} %bitcast.15, f32[48,40,128]{2,1,0:T(8,128)} %bitcast.8, ...), custom_call_target="tpu_custom_call" | custom-call | tf_op jit(solution)/shard_map/exchange_and_solve/pallas_call | solution.py:418

commit v3 on v2

--- a/solution.py
+++ b/solution.py
@@ -92,17 +92,20 @@
     def flow(first, slots, send, recv):
         def copy(slot, d):
             if slot == 0:
-                src, target = first, y_to[d]
-            elif slot <= right_steps:
-                before = slot - 1
-                src = first if before == 0 and d == 0 else slots.at[before, d]
-                target = z_right
+                src, dst, target = first, slots.at[0, d], y_to[d]
             else:
-                before = (slot + 1) % z_count
-                src = first if before == 0 and d == 0 else slots.at[before, d]
-                target = z_left
+                if slot <= right_steps:
+                    before, target = slot - 1, z_right
+                else:
+                    before, target = (slot + 1) % z_count, z_left
+                if d == 0:
+                    src = first if before == 0 else slots.at[before, 0]
+                    dst = slots.at[slot, 0]
+                else:
+                    src = slots.at[before, 1:Y_GROUPS]
+                    dst = slots.at[slot, 1:Y_GROUPS]
             return pltpu.make_async_remote_copy(
-                src_ref=src, dst_ref=slots.at[slot, d], send_sem=send.at[slot, d],
+                src_ref=src, dst_ref=dst, send_sem=send.at[slot, d],
                 recv_sem=recv.at[slot, d], device_id=target, device_id_type=mesh_ids,
             )
 
@@ -121,10 +124,11 @@
 
     def advance(copy, step, d):
         if step == 0:
-            if d > 0:
-                copy(0, d).wait_recv()
-                copy(1, d).start()
-                copy(z_count - 1, d).start()
+            if d:
+                for group in range(1, Y_GROUPS):
+                    copy(0, group).wait_recv()
+                copy(1, 1).start()
+                copy(z_count - 1, 1).start()
             return
         copy(step, d).wait_recv()
         if step < right_steps:
@@ -135,18 +139,19 @@
                 copy(z_count - step - 1, d).start()
 
     order = []
-    for d in range(Y_GROUPS):
-        delay = 0.5 + 0.7 * min(d, Y_GROUPS - d) if d else 0.0
+    for d in (0, 1):
+        delay = 1.5 * d
         for step in range(right_steps + 1):
             order.append((step + delay, d, step, False))
             order.append((step + delay + 0.6, d, step, True))
     order.sort()
 
     def finish(copy):
-        for slot in range(z_count):
-            for d in range(Y_GROUPS):
-                if slot or d:
-                    copy(slot, d).wait_send()
+        for group in range(1, Y_GROUPS):
+            copy(0, group).wait_send()
+        for slot in range(1, z_count):
+            copy(slot, 0).wait_send()
+            copy(slot, 1).wait_send()
 
     for edge in edges:
         edge.start()
@@ -190,8 +195,8 @@
 
 
 def main_kernel(
-    tr, es, ns, mix, om, fold, gat, top_rows, from_south, from_north, from_west, from_east,
-    cell, atm, owner, weight, out, table, total, mirror,
+    tr, es, ns, mix, om, fold, gat, top_all, from_south, from_north, from_west, from_east,
+    cell, atm, owner, weight, out, table, total, mirror, top_rows, top_sem,
 ):
     tracer_count, level_count, row_count, cols = tr.shape
     lon_count = gat.shape[0]
@@ -207,6 +212,12 @@
     lat_count = lax.axis_size("lat")
     is_top = lax.axis_index("lat") == lat_count - 1
     is_bottom = lax.axis_index("lat") == 0
+
+    top_copy = pltpu.make_async_copy(top_all, top_rows, top_sem)
+
+    @pl.when(is_top)
+    def _():
+        top_copy.start()
 
     def place_of(owners):
         y = jnp.zeros_like(owners)
@@ -269,6 +280,7 @@
 
     @pl.when(is_top)
     def _():
+        top_copy.wait()
         depth = FOLD_STEP * LANES
         lane_row = lax.broadcasted_iota(jnp.int32, (depth, LANES), 0)
         pad = mirror.shape[0]
@@ -379,6 +391,7 @@
     north_pad = -(-(plane_count + 1 + level_count) // 8) * 8
     f32 = jnp.float32
     vmem = pl.BlockSpec(memory_space=pltpu.VMEM)
+    anywhere = pl.BlockSpec(memory_space=pl.ANY)
     edges = (
         jax.ShapeDtypeStruct((north_pad, cols), f32),
         jax.ShapeDtypeStruct((pad, cols), f32),
@@ -401,7 +414,7 @@
             jax.ShapeDtypeStruct(spots + (pad, cols), f32),
         ) + edges,
         in_specs=[vmem] * 5,
-        out_specs=(vmem,) * 6,
+        out_specs=(vmem, anywhere) + (vmem,) * 4,
         scratch_shapes=[
             pltpu.SemaphoreType.DMA(spots),
             pltpu.SemaphoreType.DMA(spots),
@@ -418,12 +431,14 @@
     return pl.pallas_call(
         main_kernel,
         out_shape=jax.ShapeDtypeStruct(tracers.shape, f32),
-        in_specs=[vmem] * 16,
+        in_specs=[vmem] * 7 + [anywhere] + [vmem] * 8,
         out_specs=vmem,
         scratch_shapes=[
             pltpu.VMEM(((tracer_count + 1) * LANES, 2 * lon_count * blocks), jnp.bfloat16),
             pltpu.VMEM((2 * (tracer_count + 1) * row_count, cols), f32),
             pltpu.VMEM((pad, cols), f32),
+            pltpu.VMEM((lon_count, pad, cols), f32),
+            pltpu.SemaphoreType.DMA(()),
         ],
         name="exchange_and_solve",
     )(

time: 59.4 us -> 59.1 us (level)
  the two profiles are of different devices: /device:TPU:6 before, /device:TPU:14 now
where the time goes in v3:
time: 59.1 us; the launch traced here: 58.8 us
  Pallas kernels  58.8 us (99%)
    pallas_call x1, Pallas kernels, body(): pl.pallas_call(exchange_kernel, out_shape=(jax.ShapeDtypeStruct(spots + (...  45.6 us
    pallas_call x1, Pallas kernels, body(): pl.pallas_call(main_kernel, out_shape=jax.ShapeDtypeStruct(tracers.shape,...  11.3 us
    pallas_call x1, Pallas kernels, body(): pl.pallas_call(pack_kernel, out_shape=(jax.ShapeDtypeStruct((base, cols),...  1.89 us

profile of v3, /device:TPU:14, one launch (start us, length us, event | category | flops | bytes accessed | tf_op | source)
XLA Modules:
  0.0 58.8 jit_solution(347058191275566110)
XLA Ops:
  0.0 1.9 %pack_edges.1 = (f32[40,128]{1,0:T(8,128)}, f32[48,128]{1,0:T(8,128)}, f32[40,128]{1,0:T(8,128)}, f32[16,128]{1,0:T(8,128)}, f32[16,128]{1,0:T(8,128)}) custom-call(f32[4,8,16,128]{3,2,1,0:T(8,128)} %tr.3, f32[8,16,128]{2,1,0:T(8,128)} %es.3, f32[8,16,128]{2,1,0:T(8,128)} %ns.3, s32[16,128]{1,0:T(8,128)} %om.3, f32[4,1024]{1,0:T(4,128)} %state.1, ...), custom_call_target="tpu_custom_call" | custom-call | tf_op jit(solution)/shard_map/pack_edges/pallas_call | solution.py:401
  1.9 45.6 %exchange_edges.1 = (f32[12,4,40,128]{3,2,1,0:T(8,128)}, f32[12,4,40,128]{3,2,1,0:T(8,128)}, f32[48,128]{1,0:T(8,128)}, f32[40,128]{1,0:T(8,128)}, f32[16,128]{1,0:T(8,128)}, /*index=5*/f32[16,128]{1,0:T(8,128)}) custom-call(f32[40,128]{1,0:T(8,128)} %get-tuple-element.16.air, f32[48,128]{1,0:T(8,128)} %get-tuple-element.17.north, ...), custom_call_target="tpu_custom_call" | custom-call | tf_op jit(solution)/shard_map/exchange_edges/pallas_call | solution.py:410
  47.5 11.3 %exchange_and_solve.1 = f32[4,8,16,128]{3,2,1,0:T(8,128)} custom-call(f32[4,8,16,128]{3,2,1,0:T(8,128)} %tr.3, f32[8,16,128]{2,1,0:T(8,128)} %es.3, f32[8,16,128]{2,1,0:T(8,128)} %ns.3, f32[7,16,128]{2,1,0:T(8,128)} %mix.1, s32[16,128]{1,0:T(8,128)} %om.3, s32[1,128]{1,0:T(1,128)} %bitcast.15, f32[48,40,128]{2,1,0:T(8,128)} %bitcast.8, ...), custom_call_target="tpu_custom_call" | custom-call | tf_op jit(solution)/shard_map/exchange_and_solve/pallas_call | solution.py:431

commit v4 on v3

--- a/solution.py
+++ b/solution.py
@@ -12,7 +12,7 @@
 Y_GROUPS = 4
 
 
-def pack_kernel(tr, es, ns, om, state, coef, air, north, south, east, west):
+def pack_edges(tr, es, ns, om, state, coef, air, north, south, east, west):
     tracer_count, level_count, row_count, cols = tr.shape
     blocks = state.shape[1] // LANES
     for t in range(tracer_count):
@@ -46,8 +46,9 @@
 
 
 def exchange_kernel(
+    tr, es, ns, om, state, coef,
+    air_all, top_all, from_south, from_north, from_west, from_east,
     air, north, south, east, west,
-    air_all, top_all, from_south, from_north, from_west, from_east,
     send_air, recv_air, send_top, recv_top, send_edge, recv_edge, own,
 ):
     z_count = air_all.shape[0]
@@ -71,6 +72,7 @@
     barrier = pltpu.get_barrier_semaphore()
     for partner in partners:
         pl.semaphore_signal(barrier, inc=1, device_id=partner, device_id_type=mesh_ids)
+    pack_edges(tr, es, ns, om, state, coef, air, north, south, east, west)
     pl.semaphore_wait(barrier, len(partners))
 
     edges = []
@@ -398,24 +400,22 @@
         jax.ShapeDtypeStruct((row_count, cols), f32),
         jax.ShapeDtypeStruct((row_count, cols), f32),
     )
-    air, north, south, east, west = pl.pallas_call(
-        pack_kernel,
-        out_shape=(jax.ShapeDtypeStruct((base, cols), f32),) + edges,
-        in_specs=[vmem] * 6,
-        out_specs=(vmem,) * 5,
-        name="pack_edges",
-    )(tracers, east_speed, north_speed, ocean_mask, atmos_state, atmos_coef.reshape(blocks, LANES))
     z_count = lon_count // Y_GROUPS
     spots = (z_count, Y_GROUPS)
     air_all, top_all, from_south, from_north, from_west, from_east = pl.pallas_call(
         exchange_kernel,
         out_shape=(
-            jax.ShapeDtypeStruct(spots + (base, cols), f32),
+            pltpu.VMEM(spots + (base, cols), f32),
             jax.ShapeDtypeStruct(spots + (pad, cols), f32),
         ) + edges,
-        in_specs=[vmem] * 5,
+        in_specs=[vmem] * 6,
         out_specs=(vmem, anywhere) + (vmem,) * 4,
         scratch_shapes=[
+            pltpu.VMEM((base, cols), f32),
+            pltpu.VMEM((north_pad, cols), f32),
+            pltpu.VMEM((pad, cols), f32),
+            pltpu.VMEM((row_count, cols), f32),
+            pltpu.VMEM((row_count, cols), f32),
             pltpu.SemaphoreType.DMA(spots),
             pltpu.SemaphoreType.DMA(spots),
             pltpu.SemaphoreType.DMA(spots),
@@ -426,7 +426,7 @@
         ],
         compiler_params=pltpu.CompilerParams(collective_id=0, has_side_effects=True),
         name="exchange_edges",
-    )(air, north, south, east, west)
+    )(tracers, east_speed, north_speed, ocean_mask, atmos_state, atmos_coef.reshape(blocks, LANES))
     rows = xgrid_cell.shape[0] // LANES
     return pl.pallas_call(
         main_kernel,

time: 59.1 us -> 57.9 us (0.980)
  Pallas kernels: 58.8 us -> 56.8 us
  local copies, waits for them, and re-layouts: 0 us -> 0.98 us
    pallas_call x2 -> x1, Pallas kernels: 47.5 us -> 45.5 us  [body(): pl.pallas_call(exchange_kernel, out_shape=(pltpu.VMEM(spots + (base, cols...]
    unnamed x0 -> x2, local copies, waits for them, and re-layouts: none -> 0.98 us
where the time goes in v4:
time: 57.9 us; the launch traced here: 57.8 us
  Pallas kernels  56.8 us (98%)
  local copies, waits for them, and re-layouts  0.98 us (2%)
    pallas_call x1, Pallas kernels, body(): pl.pallas_call(exchange_kernel, out_shape=(pltpu.VMEM(spots + (base, cols...  45.5 us
    pallas_call x1, Pallas kernels, body(): pl.pallas_call(main_kernel, out_shape=jax.ShapeDtypeStruct(tracers.shape,...  11.3 us

profile of v4, /device:TPU:14, one launch (start us, length us, event | category | flops | bytes accessed | tf_op | source)
XLA Modules:
  0.0 57.8 jit_solution(9507552789546630026)
XLA Ops:
  0.0 45.5 %exchange_edges.1 = (f32[12,4,40,128]{3,2,1,0:T(8,128)S(1)}, f32[12,4,40,128]{3,2,1,0:T(8,128)}, f32[48,128]{1,0:T(8,128)}, f32[40,128]{1,0:T(8,128)}, f32[16,128]{1,0:T(8,128)}, /*index=5*/f32[16,128]{1,0:T(8,128)}) custom-call(f32[4,8,16,128]{3,2,1,0:T(8,128)} %tr.3, f32[8,16,128]{2,1,0:T(8,128)} %es.3, f32[8,16,128]{2,1,0:T(8,128)} %ns.3, s32[16,128]{1,0:T(8,128)} %om.3, ...), custom_call_target="tpu_custom_call" | custom-call | tf_op jit(solution)/shard_map/exchange_edges/pallas_call | solution.py:405
  45.5 0.0 copy-start
  45.5 1.0 %copy-done = f32[12,4,40,128]{3,2,1,0:T(8,128)} copy-done((f32[12,4,40,128]{3,2,1,0:T(8,128)}, f32[12,4,40,128]{3,2,1,0:T(8,128)S(1)}, u32[]{:S(2)}) %copy-start) | copy-done | bytes 983064
  46.5 11.3 %exchange_and_solve.1 = f32[4,8,16,128]{3,2,1,0:T(8,128)} custom-call(f32[4,8,16,128]{3,2,1,0:T(8,128)} %tr.3, f32[8,16,128]{2,1,0:T(8,128)} %es.3, f32[8,16,128]{2,1,0:T(8,128)} %ns.3, f32[7,16,128]{2,1,0:T(8,128)} %mix.1, s32[16,128]{1,0:T(8,128)} %om.3, s32[1,128]{1,0:T(1,128)} %bitcast.15, f32[48,40,128]{2,1,0:T(8,128)} %bitcast.8, ...), custom_call_target="tpu_custom_call" | custom-call | tf_op jit(solution)/shard_map/exchange_and_solve/pallas_call | solution.py:431
Async XLA Ops:
  45.5 1.0 %copy-start = (f32[12,4,40,128]{3,2,1,0:T(8,128)}, f32[12,4,40,128]{3,2,1,0:T(8,128)S(1)}, u32[]{:S(2)}) copy-start(f32[12,4,40,128]{3,2,1,0:T(8,128)S(1)} %get-tuple-element.11) | copy-start | bytes 2949124

commit v5 on v4

--- a/solution.py
+++ b/solution.py
@@ -443,7 +443,8 @@
         name="exchange_and_solve",
     )(
         tracers, east_speed, north_speed, mixing_coef, ocean_mask, fold_map.reshape(1, cols),
-        air_all.reshape(lon_count, base, cols), top_all.reshape(lon_count, pad, cols), from_south, from_north, from_west, from_east,
+        pltpu.with_memory_space_constraint(air_all.reshape(lon_count, base, cols), pltpu.VMEM),
+        top_all.reshape(lon_count, pad, cols), from_south, from_north, from_west, from_east,
         xgrid_cell.reshape(rows, LANES), xgrid_atm.reshape(rows, LANES),
         xgrid_owner.reshape(rows, LANES), xgrid_weight.reshape(rows, LANES),
     )

time: 57.9 us -> 56.6 us (0.978)
  local copies, waits for them, and re-layouts: 0.98 us -> 0 us
    unnamed x2 -> x0, local copies, waits for them, and re-layouts: 0.98 us -> none
where the time goes in v5:
time: 56.6 us; the launch traced here: 56.5 us
  Pallas kernels  56.5 us (100%)
    pallas_call x1, Pallas kernels, body(): pl.pallas_call(exchange_kernel, out_shape=(pltpu.VMEM(spots + (base, cols...  45.5 us
    pallas_call x1, Pallas kernels, body(): pl.pallas_call(main_kernel, out_shape=jax.ShapeDtypeStruct(tracers.shape,...  11 us

profile of v5, /device:TPU:14, one launch (start us, length us, event | category | flops | bytes accessed | tf_op | source)
XLA Modules:
  0.0 56.5 jit_solution(4185435925991863408)
XLA Ops:
  0.0 45.5 %exchange_edges.1 = (f32[12,4,40,128]{3,2,1,0:T(8,128)S(1)}, f32[12,4,40,128]{3,2,1,0:T(8,128)}, f32[48,128]{1,0:T(8,128)}, f32[40,128]{1,0:T(8,128)}, f32[16,128]{1,0:T(8,128)}, /*index=5*/f32[16,128]{1,0:T(8,128)}) custom-call(f32[4,8,16,128]{3,2,1,0:T(8,128)} %tr.3, f32[8,16,128]{2,1,0:T(8,128)} %es.3, f32[8,16,128]{2,1,0:T(8,128)} %ns.3, s32[16,128]{1,0:T(8,128)} %om.3, ...), custom_call_target="tpu_custom_call" | custom-call | tf_op jit(solution)/shard_map/exchange_edges/pallas_call | solution.py:405
  45.5 11.0 %exchange_and_solve.1 = f32[4,8,16,128]{3,2,1,0:T(8,128)} custom-call(f32[4,8,16,128]{3,2,1,0:T(8,128)} %tr.3, f32[8,16,128]{2,1,0:T(8,128)} %es.3, f32[8,16,128]{2,1,0:T(8,128)} %ns.3, f32[7,16,128]{2,1,0:T(8,128)} %mix.1, s32[16,128]{1,0:T(8,128)} %om.3, s32[1,128]{1,0:T(1,128)} %bitcast.15, f32[48,40,128]{2,1,0:T(8,128)S(1)} %bitcast.8, ...), custom_call_target="tpu_custom_call" | custom-call | tf_op jit(solution)/shard_map/exchange_and_solve/pallas_call | solution.py:431
